TPU v7x, 32 devices: a whole 2x2x4 slice. The times are simulated.
32 devices in a mesh: groups: 2 (over y), frame: 4 (over z), panel: 2 (over x), sub: 2 (over core).
Axes of the slice: x: 2, y: 2, z: 4, core: 2. Of those that a mesh axis runs over, the one named last changes fastest.
Arguments:
- frames: bfloat16 [2048, 65536], P(('groups', 'frame'), ('panel', 'sub')), parts along dimension 0, may hold values from -16 to 16
- slices: float32 [32, 65536], P(('groups', 'frame'), ('panel', 'sub')), parts along dimension 0, may hold values from -8 to 8
- log_prior: float32 [4096], replicated, may hold values from -2 to 2
- orient: int32 [32], P('groups'), parts along dimension 0, may hold values from 0 to 4095
Outputs:
- new_slices: float32 [32, 65536], P(('groups', 'frame'), ('panel', 'sub')), parts along dimension 0
There are 2 independent parts, one for each index of `groups`. A program takes and returns all parts, laid end to end along the dimension named above; an argument that names none is the same for every part. Nothing has to cross between parts.
All inputs are finite; a program needn't handle non-finite values.
Results may differ from a plain program's by a relative error of at most 0.022.
The roundings to bfloat16 on the way count: a program that leaves them out, or rounds other values in their place, can miss the bound.
Values may be sent and summed in bfloat16 or wider, within the bound.
A program may use at most 64 MiB of HBM per device.

v0:
```python
import math
import jax
import jax.numpy as jnp
from jax import lax
from jax.sharding import PartitionSpec as P

PIX = 65536
ITERS = 2


def fetch_slices(owned_b):
    return lax.all_gather(owned_b, "frame", axis=0, tiled=True)


def owner_update(weights, frames, counts, owned_b, offset):
    owned = owned_b.shape[0]
    mine = lax.psum_scatter(
        jnp.einsum("fm,fp->mp", weights, frames, preferred_element_type=jnp.float32).astype(
            jnp.bfloat16
        ),
        "frame",
        scatter_dimension=0,
        tiled=True,
    ).astype(jnp.float32)
    my_counts = lax.dynamic_slice_in_dim(counts, offset, owned, 0)
    return (mine + owned_b.astype(jnp.float32)) / (my_counts + 1.0)[:, None]


def local(frames, slices, log_prior, orient):
    owned = slices.shape[0]
    temper = 3.0 / math.sqrt(PIX)
    matches = orient[:, None] == jnp.arange(log_prior.shape[0], dtype=jnp.int32)[None, :]
    prior = jnp.sum(jnp.where(matches, log_prior[None, :], 0.0), axis=1)
    offset = lax.axis_index("frame") * owned
    current = slices
    owned_b = slices.astype(jnp.bfloat16)
    for step in range(ITERS):
        if step == 0:
            gathered = fetch_slices(owned_b)
        else:
            gathered = fetch_slices(owned_b)
        wide = gathered.astype(jnp.float32)
        norms = jnp.sum(wide * wide, axis=1)
        raw = (
            jnp.einsum("fp,mp->fm", frames, gathered, preferred_element_type=jnp.float32)
            - 0.5 * norms[None, :]
        )
        summed = lax.psum(raw, ("panel", "sub"))
        weights = jax.nn.softmax(temper * summed + prior[None, :], axis=1).astype(jnp.bfloat16)
        counts = lax.psum(jnp.sum(weights.astype(jnp.float32), axis=0), "frame")
        if step + 1 < ITERS:
            current = owner_update(weights, frames, counts, owned_b, offset)
            owned_b = current.astype(jnp.bfloat16)
        else:
            current = owner_update(weights, frames, counts, owned_b, offset)
    return current


def solution(mesh):
    in_specs = (
        P(("groups", "frame"), ("panel", "sub")),
        P(("groups", "frame"), ("panel", "sub")),
        P(),
        P("groups"),
    )
    out_specs = P(("groups", "frame"), ("panel", "sub"))
    return jax.shard_map(local, mesh=mesh, in_specs=in_specs, out_specs=out_specs, check_vma=False)
```

profile of v0, /device:TPU:0, one launch (start us, length us, event | category | flops | bytes accessed | tf_op | source)
XLA Modules:
  0.0 173.9 jit_solution(4613914813418080331)
XLA Ops:
  6.5 1.0 convert_bitcast_fusion
  7.6 17.4 %all-gather = bf16[4,4,16384]{2,1,0:T(4,128)(2,1)S(1)} all-gather(bf16[1,4,16384]{2,1,0:T(4,128)(2,1)S(1)} %convert_bitcast_fusion), channel_id=1, replica_groups=mesh['groups'=2,'frame'=4,'panel'=2,'sub'=2] {'frame'}, dimensions={0}, use_global_device_ids=true | all-gather | bytes 655360 | tf_op jit(solution)/shard_map/all_gather | solution.py:12
  24.9 0.1 reshape.18
  25.1 0.2 multiply_reduce_fusion.1
  25.3 5.7 %convolution_subtract_fusion.1 = f32[256,16]{0,1:T(8,128)S(1)} fusion(bf16[256,16384]{1,0:T(8,128)(2,1)} %param.4, bf16[16,16384]{1,0:T(8,128)(2,1)S(1)} %reshape.18, f32[16]{0:T(128)S(1)} %broadcast_multiply_fusion.1), kind=kOutput, calls=%fused_computation.4 | convolution fusion | flops 134221824 | bytes 8929344 | tf_op jit(solution)/shard_map/fp,mp->fm/dot_general | solution.py:45
  31.0 10.1 %psum.28 = f32[256,16]{0,1:T(8,128)S(1)} all-reduce(f32[256,16]{0,1:T(8,128)S(1)} %convolution_subtract_fusion.1), channel_id=1, replica_groups=mesh['groups'=2,'frame'=4,'panel'=2,'sub'=2] {'panel','sub'}, use_global_device_ids=true, to_apply=%region_1.2 | all-reduce | flops 4096 | bytes 32768 | tf_op jit(solution)/shard_map/psum | solution.py:48
  41.1 0.2 select_reduce_fusion
  41.5 0.1 fusion.4
  41.6 0.2 convert_reduce_fusion.1
  41.7 5.4 %convolution_convert_fusion.1 = bf16[16,16384]{1,0:T(8,128)(2,1)} fusion(bf16[256,16]{0,1:T(8,128)(2,1)S(1)} %get-tuple-element.8, bf16[256,16384]{1,0:T(8,128)(2,1)} %param.4), kind=kOutput, calls=%fused_computation.1 | convolution fusion | flops 134479872 | bytes 8921088 | tf_op jit(solution)/shard_map/fm,fp->mp/dot_general | solution.py:18
  47.3 0.6 dynamic-slice
  48.5 12.6 %psum.29 = f32[16]{0:T(128)S(1)} all-reduce(f32[16]{0:T(128)S(1)} %get-tuple-element.7), channel_id=1, replica_groups=mesh['groups'=2,'frame'=4,'panel'=2,'sub'=2] {'frame'}, use_global_device_ids=true, to_apply=%region_7.8 | all-reduce | flops 16 | bytes 128 | tf_op jit(solution)/shard_map/psum | solution.py:50
  61.1 26.4 %all-reduce.5.cloned.1.call-done = bf16[16,16384]{1,0:T(8,128)(2,1)} async-done(((bf16[16,16384]{1,0:T(8,128)(2,1)}), bf16[16,16384]{1,0:T(8,128)(2,1)}) %all-reduce.5.cloned.1.call-update) | async-done | bytes 524304
  87.6 1.1 fusion.1
  88.6 16.2 %all-gather.1 = bf16[4,4,16384]{2,1,0:T(4,128)(2,1)S(1)} all-gather(bf16[1,4,16384]{2,1,0:T(4,128)(2,1)S(1)} %bitcast.14), channel_id=1, replica_groups=mesh['groups'=2,'frame'=4,'panel'=2,'sub'=2] {'frame'}, dimensions={0}, use_global_device_ids=true | all-gather | bytes 655360 | tf_op jit(solution)/shard_map/all_gather | solution.py:12
  104.8 0.1 reshape.20
  104.9 0.2 multiply_reduce_fusion
  105.2 5.6 %fusion = f32[256,16]{0,1:T(8,128)S(1)} fusion(bf16[16,16384]{1,0:T(8,128)(2,1)S(1)} %reshape.20, bf16[256,16384]{1,0:T(8,128)(2,1)} %param.4, f32[16]{0:T(128)S(1)} %broadcast_multiply_fusion), kind=kOutput, calls=%fused_computation.3 | convolution fusion | flops 134221824 | bytes 8929344 | tf_op jit(solution)/shard_map/fp,mp->fm/dot_general | solution.py:45
  110.8 10.1 %psum.30 = f32[256,16]{0,1:T(8,128)S(1)} all-reduce(f32[256,16]{0,1:T(8,128)S(1)} %fusion), channel_id=1, replica_groups=mesh['groups'=2,'frame'=4,'panel'=2,'sub'=2] {'panel','sub'}, use_global_device_ids=true, to_apply=%region_9.10 | all-reduce | flops 4096 | bytes 32768 | tf_op jit(solution)/shard_map/psum | solution.py:48
  121.1 0.2 convert_reduce_fusion
  121.3 5.4 %convolution_convert_fusion = bf16[16,16384]{1,0:T(8,128)(2,1)} fusion(bf16[256,16]{0,1:T(8,128)(2,1)S(1)} %get-tuple-element.6, bf16[256,16384]{1,0:T(8,128)(2,1)} %param.4), kind=kOutput, calls=%fused_computation | convolution fusion | flops 134479872 | bytes 8921088 | tf_op jit(solution)/shard_map/fm,fp->mp/dot_general | solution.py:18
  126.7 10.8 %psum.31 = f32[16]{0:T(128)S(1)} all-reduce(f32[16]{0:T(128)S(1)} %get-tuple-element.5), channel_id=1, replica_groups=mesh['groups'=2,'frame'=4,'panel'=2,'sub'=2] {'frame'}, use_global_device_ids=true, to_apply=%region_14.15 | all-reduce | flops 16 | bytes 128 | tf_op jit(solution)/shard_map/psum | solution.py:50
  137.6 27.7 %all-reduce.7.cloned.1.call-done = bf16[16,16384]{1,0:T(8,128)(2,1)} async-done(((bf16[16,16384]{1,0:T(8,128)(2,1)}), bf16[16,16384]{1,0:T(8,128)(2,1)}) %all-reduce.7.cloned.1.call-update) | async-done | bytes 524304
  165.3 1.8 %add_divide_fusion = f32[4,16384]{1,0:T(4,128)} fusion(bf16[4,16384]{1,0:T(4,128)(2,1)S(1)} %fusion.1, bf16[16,16384]{1,0:T(8,128)(2,1)} %all-reduce.7.cloned.1.call-done, u32[]{:T(128)S(6)} %multiply.1, f32[4]{0:T(128)S(1)} %dynamic-slice_add_fusion), kind=kLoop, calls=%fused_computation.7 | loop fusion | flops 262144 | bytes 524308 | tf_op jit(solution)/shard_map/div | solution.py:26
  (19 shorter events, 0.5 us)
Async XLA Ops:
  6.5 34.6 %copy-start.2 = (s32[16]{0:T(128)S(1)}, s32[16]{0:T(128)}, u32[]{:S(2)}) copy-start(s32[16]{0:T(128)} %param.7) | copy-start | bytes 196
  6.5 34.6 %copy-start.1 = (f32[4096]{0:T(1024)S(1)}, f32[4096]{0:T(1024)}, u32[]{:S(2)}) copy-start(f32[4096]{0:T(1024)} %param.6) | copy-start | bytes 49156
  6.5 81.0 %all-reduce.5.cloned.1.call-start = ((), (), s32[]{:S(2)}) async-start(), calls=%async_computation | async-start | bytes 1048576
  25.3 21.9 %copy-start.3 = (u32[32]{0:T(128)S(1)}, u32[32]{0:T(128)}, u32[]{:S(2)}) copy-start(u32[32]{0:T(128)} %constant.25) | copy-start | bytes 388
  25.3 62.2 %copy-start = (f32[4,16384]{1,0:T(4,128)S(1)}, f32[4,16384]{1,0:T(4,128)}, u32[]{:S(2)}) copy-start(f32[4,16384]{1,0:T(4,128)} %param.5) | copy-start | bytes 786436
  47.2 118.2 %all-reduce.7.cloned.1.call-start = ((), (), s32[]{:S(2)}) async-start(), calls=%async_computation.1 | async-start | bytes 1048576
Sparse Core Ops, SparseCore 0:
  47.3 40.1 all-reduce.4
  126.9 38.4 all-reduce.6
where the time goes:
time: 174 us
  blocking collectives  77.1 us (44%)
  waiting for transfers between devices  54.2 us (31%)
  matrix products  22.2 us (13%)
  between operations  14.1 us (8%)
  other arithmetic  5.48 us (3%)
    unnamed x4, waiting for transfers between devices  54.2 us
    all_gather x2, blocking collectives, fetch_slices(): return lax.all_gather(owned_b, 'frame', axis=0, tiled=True)  33.5 us
    psum x2, blocking collectives, local(): counts = lax.psum(jnp.sum(weights.astype(jnp.float32), axis=0), 'frame')  23.3 us
    psum x2, blocking collectives, local(): summed = lax.psum(raw, ('panel', 'sub'))  20.2 us
    dot_general x2, matrix products, local(): jnp.einsum('fp,mp->fm', frames, gathered, preferred_element_type=jnp.floa...  11.3 us
    dot_general x2, matrix products, owner_update(): jnp.einsum('fm,fp->mp', weights, frames, preferred_element_type=jnp.float32)  10.8 us
  transfers between devices with their start and end apart: 2, of which 2 were waited for; matrix products, arithmetic and copies ran while one was open for 0% of the time, Pallas kernels for 0%

commit v1 on v0

--- a/solution.py
+++ b/solution.py
@@ -45,7 +45,7 @@
             jnp.einsum("fp,mp->fm", frames, gathered, preferred_element_type=jnp.float32)
             - 0.5 * norms[None, :]
         )
-        summed = lax.psum(raw, ("panel", "sub"))
+        summed = lax.psum(lax.psum(raw, "panel"), "sub")
         weights = jax.nn.softmax(temper * summed + prior[None, :], axis=1).astype(jnp.bfloat16)
         counts = lax.psum(jnp.sum(weights.astype(jnp.float32), axis=0), "frame")
         if step + 1 < ITERS:

time: 174 us -> 175 us (level)
  blocking collectives: 77.1 us -> 80 us
  waiting for transfers between devices: 54.2 us -> 52.1 us
    psum x2 -> x4, blocking collectives: 20.2 us -> 22.7 us  [local(): summed = lax.psum(lax.psum(raw, 'panel'), 'sub')]
    unnamed x4, waiting for transfers between devices: 54.2 us -> 52.1 us
where the time goes in v1:
time: 175 us
  blocking collectives  80 us (46%)
  waiting for transfers between devices  52.1 us (30%)
  matrix products  22.2 us (13%)
  between operations  14.1 us (8%)
  other arithmetic  5.48 us (3%)
    unnamed x4, waiting for transfers between devices  52.1 us
    all_gather x2, blocking collectives, fetch_slices(): return lax.all_gather(owned_b, 'frame', axis=0, tiled=True)  33.5 us
    psum x2, blocking collectives, local(): counts = lax.psum(jnp.sum(weights.astype(jnp.float32), axis=0), 'frame')  23.7 us
    psum x4, blocking collectives, local(): summed = lax.psum(lax.psum(raw, 'panel'), 'sub')  22.7 us
    dot_general x2, matrix products, local(): jnp.einsum('fp,mp->fm', frames, gathered, preferred_element_type=jnp.floa...  11.3 us
    dot_general x2, matrix products, owner_update(): jnp.einsum('fm,fp->mp', weights, frames, preferred_element_type=jnp.float32)  10.8 us
  transfers between devices with their start and end apart: 2, of which 2 were waited for; matrix products, arithmetic and copies ran while one was open for 0% of the time, Pallas kernels for 0%

profile of v1, /device:TPU:0, one launch (start us, length us, event | category | flops | bytes accessed | tf_op | source)
XLA Modules:
  0.0 174.7 jit_solution(5448121330955539216)
XLA Ops:
  6.5 1.0 convert_bitcast_fusion
  7.6 17.4 %all-gather = bf16[4,4,16384]{2,1,0:T(4,128)(2,1)S(1)} all-gather(bf16[1,4,16384]{2,1,0:T(4,128)(2,1)S(1)} %convert_bitcast_fusion), channel_id=1, replica_groups=mesh['groups'=2,'frame'=4,'panel'=2,'sub'=2] {'frame'}, dimensions={0}, use_global_device_ids=true | all-gather | bytes 655360 | tf_op jit(solution)/shard_map/all_gather | solution.py:12
  25.1 0.2 multiply_reduce_fusion.1
  25.3 5.7 %convolution_subtract_fusion.1 = f32[256,16]{0,1:T(8,128)S(1)} fusion(bf16[256,16384]{1,0:T(8,128)(2,1)} %param.4, bf16[16,16384]{1,0:T(8,128)(2,1)S(1)} %reshape.18, f32[16]{0:T(128)S(1)} %broadcast_multiply_fusion.1), kind=kOutput, calls=%fused_computation.4 | convolution fusion | flops 134221824 | bytes 8929344 | tf_op jit(solution)/shard_map/fp,mp->fm/dot_general | solution.py:45
  31.0 8.2 %psum.42 = f32[256,16]{0,1:T(8,128)S(1)} all-reduce(f32[256,16]{0,1:T(8,128)S(1)} %convolution_subtract_fusion.1), channel_id=1, replica_groups=mesh['groups'=2,'frame'=4,'panel'=2,'sub'=2] {'panel'}, use_global_device_ids=true, to_apply=%region_1.2 | all-reduce | flops 4096 | bytes 32768 | tf_op jit(solution)/shard_map/psum | solution.py:48
  39.2 3.3 %psum.43 = f32[256,16]{0,1:T(8,128)S(1)} all-reduce(f32[256,16]{0,1:T(8,128)S(1)} %psum.42), channel_id=1, replica_groups=mesh['groups'=2,'frame'=4,'panel'=2,'sub'=2] {'sub'}, use_global_device_ids=true, to_apply=%region_2.3 | all-reduce | flops 4096 | bytes 32768 | tf_op jit(solution)/shard_map/psum | solution.py:48
  42.5 0.2 select_reduce_fusion
  43.0 0.2 convert_reduce_fusion.1
  43.1 5.4 %convolution_convert_fusion.1 = bf16[16,16384]{1,0:T(8,128)(2,1)} fusion(bf16[256,16]{0,1:T(8,128)(2,1)S(1)} %get-tuple-element.8, bf16[256,16384]{1,0:T(8,128)(2,1)} %param.4), kind=kOutput, calls=%fused_computation.1 | convolution fusion | flops 134479872 | bytes 8921088 | tf_op jit(solution)/shard_map/fm,fp->mp/dot_general | solution.py:18
  48.6 0.6 dynamic-slice
  49.9 12.6 %psum.44 = f32[16]{0:T(128)S(1)} all-reduce(f32[16]{0:T(128)S(1)} %get-tuple-element.7), channel_id=1, replica_groups=mesh['groups'=2,'frame'=4,'panel'=2,'sub'=2] {'frame'}, use_global_device_ids=true, to_apply=%region_8.9 | all-reduce | flops 16 | bytes 128 | tf_op jit(solution)/shard_map/psum | solution.py:50
  62.5 25.4 %all-reduce.5.cloned.1.call-done = bf16[16,16384]{1,0:T(8,128)(2,1)} async-done(((bf16[16,16384]{1,0:T(8,128)(2,1)}), bf16[16,16384]{1,0:T(8,128)(2,1)}) %all-reduce.5.cloned.1.call-update) | async-done | bytes 524304
  88.0 1.1 fusion.1
  89.0 16.2 %all-gather.1 = bf16[4,4,16384]{2,1,0:T(4,128)(2,1)S(1)} all-gather(bf16[1,4,16384]{2,1,0:T(4,128)(2,1)S(1)} %bitcast.14), channel_id=1, replica_groups=mesh['groups'=2,'frame'=4,'panel'=2,'sub'=2] {'frame'}, dimensions={0}, use_global_device_ids=true | all-gather | bytes 655360 | tf_op jit(solution)/shard_map/all_gather | solution.py:12
  105.2 0.1 reshape.20
  105.3 0.2 multiply_reduce_fusion
  105.6 5.6 %fusion = f32[256,16]{0,1:T(8,128)S(1)} fusion(bf16[16,16384]{1,0:T(8,128)(2,1)S(1)} %reshape.20, bf16[256,16384]{1,0:T(8,128)(2,1)} %param.4, f32[16]{0:T(128)S(1)} %broadcast_multiply_fusion), kind=kOutput, calls=%fused_computation.3 | convolution fusion | flops 134221824 | bytes 8929344 | tf_op jit(solution)/shard_map/fp,mp->fm/dot_general | solution.py:45
  111.2 7.8 %psum.45 = f32[256,16]{0,1:T(8,128)S(1)} all-reduce(f32[256,16]{0,1:T(8,128)S(1)} %fusion), channel_id=1, replica_groups=mesh['groups'=2,'frame'=4,'panel'=2,'sub'=2] {'panel'}, use_global_device_ids=true, to_apply=%region_10.11 | all-reduce | flops 4096 | bytes 32768 | tf_op jit(solution)/shard_map/psum | solution.py:48
  119.1 3.3 %psum.46 = f32[256,16]{0,1:T(8,128)S(1)} all-reduce(f32[256,16]{0,1:T(8,128)S(1)} %psum.45), channel_id=1, replica_groups=mesh['groups'=2,'frame'=4,'panel'=2,'sub'=2] {'sub'}, use_global_device_ids=true, to_apply=%region_11.12 | all-reduce | flops 4096 | bytes 32768 | tf_op jit(solution)/shard_map/psum | solution.py:48
  122.6 0.2 convert_reduce_fusion
  122.8 5.4 %convolution_convert_fusion = bf16[16,16384]{1,0:T(8,128)(2,1)} fusion(bf16[256,16]{0,1:T(8,128)(2,1)S(1)} %get-tuple-element.6, bf16[256,16384]{1,0:T(8,128)(2,1)} %param.4), kind=kOutput, calls=%fused_computation | convolution fusion | flops 134479872 | bytes 8921088 | tf_op jit(solution)/shard_map/fm,fp->mp/dot_general | solution.py:18
  128.2 11.2 %psum.47 = f32[16]{0:T(128)S(1)} all-reduce(f32[16]{0:T(128)S(1)} %get-tuple-element.5), channel_id=1, replica_groups=mesh['groups'=2,'frame'=4,'panel'=2,'sub'=2] {'frame'}, use_global_device_ids=true, to_apply=%region_16.17 | all-reduce | flops 16 | bytes 128 | tf_op jit(solution)/shard_map/psum | solution.py:50
  139.5 26.6 %all-reduce.7.cloned.1.call-done = bf16[16,16384]{1,0:T(8,128)(2,1)} async-done(((bf16[16,16384]{1,0:T(8,128)(2,1)}), bf16[16,16384]{1,0:T(8,128)(2,1)}) %all-reduce.7.cloned.1.call-update) | async-done | bytes 524304
  166.1 1.8 %add_divide_fusion = f32[4,16384]{1,0:T(4,128)} fusion(bf16[4,16384]{1,0:T(4,128)(2,1)S(1)} %fusion.1, bf16[16,16384]{1,0:T(8,128)(2,1)} %all-reduce.7.cloned.1.call-done, u32[]{:T(128)S(6)} %multiply.1, f32[4]{0:T(128)S(1)} %dynamic-slice_add_fusion), kind=kLoop, calls=%fused_computation.7 | loop fusion | flops 262144 | bytes 524308 | tf_op jit(solution)/shard_map/div | solution.py:26
  (21 shorter events, 0.8 us)
Async XLA Ops:
  6.5 36.0 %copy-start.2 = (s32[16]{0:T(128)S(1)}, s32[16]{0:T(128)}, u32[]{:S(2)}) copy-start(s32[16]{0:T(128)} %param.7) | copy-start | bytes 196
  6.5 36.0 %copy-start.1 = (f32[4096]{0:T(1024)S(1)}, f32[4096]{0:T(1024)}, u32[]{:S(2)}) copy-start(f32[4096]{0:T(1024)} %param.6) | copy-start | bytes 49156
  6.5 81.4 %all-reduce.5.cloned.1.call-start = ((), (), s32[]{:S(2)}) async-start(), calls=%async_computation | async-start | bytes 1048576
  25.3 23.3 %copy-start.3 = (u32[32]{0:T(128)S(1)}, u32[32]{0:T(128)}, u32[]{:S(2)}) copy-start(u32[32]{0:T(128)} %constant.25) | copy-start | bytes 388
  25.3 62.7 %copy-start = (f32[4,16384]{1,0:T(4,128)S(1)}, f32[4,16384]{1,0:T(4,128)}, u32[]{:S(2)}) copy-start(f32[4,16384]{1,0:T(4,128)} %param.5) | copy-start | bytes 786436
  48.6 117.5 %all-reduce.7.cloned.1.call-start = ((), (), s32[]{:S(2)}) async-start(), calls=%async_computation.1 | async-start | bytes 1048576
Sparse Core Ops, SparseCore 0:
  48.7 39.2 all-reduce.4
  128.3 37.6 all-reduce.6
